TPU v7x, 32 devices: a whole 2x2x4 slice. The times are simulated.
32 devices in a mesh: dp: 8 (over z, x), tensor: 4 (over y, core).
Axes of the slice: x: 2, y: 2, z: 4, core: 2. Of those that a mesh axis runs over, the one named last changes fastest.
Arguments:
- tokens: bfloat16 [8192, 768], P(('dp', 'tensor')), may hold values from -6 to 6
- cotangent: bfloat16 [8192, 768], P(('dp', 'tensor')), may hold values from -6 to 6
- prefix: int32 [8], P('dp'), may hold values from 102 to 512
- w_qkv: bfloat16 [2, 3, 768, 768], P(None, None, None, 'tensor'), may hold values from -0.3125 to 0.3125
- bias_qv: float32 [2, 2, 768], P(None, None, 'tensor'), may hold values from -1.8 to 1.8
- w_out: bfloat16 [2, 768, 768], P(None, 'tensor'), may hold values from -0.625 to 0.625
- bias_out: float32 [2, 768], replicated, may hold values from -1.8 to 1.8
- norm_gain: float32 [2, 2, 768], replicated, may hold values from 0.5 to 1.5
- norm_bias: float32 [2, 2, 768], replicated, may hold values from -1.8 to 1.8
- w_up: bfloat16 [2, 768, 3072], P(None, None, 'tensor'), may hold values from -0.21875 to 0.21875
- bias_up: float32 [2, 3072], P(None, 'tensor'), may hold values from -3 to 3
- w_down: bfloat16 [2, 3072, 768], P(None, 'tensor'), may hold values from -0.15625 to 0.15625
- bias_down: float32 [2, 768], replicated, may hold values from -1.8 to 1.8
Outputs:
- output: float32 [8192, 768], P(('dp', 'tensor'))
- grad_tokens: float32 [8192, 768], P(('dp', 'tensor'))
- grad_w_qkv: float32 [2, 3, 768, 768], P(None, None, 'dp', 'tensor')
- grad_bias_qv: float32 [2, 2, 768], P(None, None, 'tensor')
- grad_w_out: float32 [2, 768, 768], P(None, 'tensor', 'dp')
- grad_bias_out: float32 [2, 768], replicated
- grad_norm_gain: float32 [2, 2, 768], replicated
- grad_norm_bias: float32 [2, 2, 768], replicated
- grad_w_up: float32 [2, 768, 3072], P(None, 'dp', 'tensor')
- grad_bias_up: float32 [2, 3072], P(None, 'tensor')
- grad_w_down: float32 [2, 3072, 768], P(None, 'tensor', 'dp')
- grad_bias_down: float32 [2, 768], replicated
All inputs are finite; a program needn't handle non-finite values.
Results may differ from a plain program's by a relative error of at most 0.025.
The roundings to bfloat16 on the way count: a program that leaves them out, or rounds other values in their place, can miss the bound.
Values may be sent and summed in bfloat16 or wider, within the bound.
A program may use at most 192 MiB of HBM per device.

v0:
```python
import functools
import math
import jax
import jax.numpy as jnp
from jax import lax
from jax.sharding import PartitionSpec as P

HDIM = 64
LEN = 1024
MEM = 10
EPSILON = 1e-06
HIGHEST = lax.Precision.HIGHEST


def gather_rows(values_in):
    return lax.all_gather(values_in, "tensor", axis=0, tiled=True)


def sum_rows(term_fn, row_count):
    return lax.psum_scatter(
        term_fn(jnp.int32(0), lax.axis_size("tensor") * row_count),
        "tensor",
        scatter_dimension=0,
        tiled=True,
    )


def gather_grad(values_in):
    return lax.all_gather(values_in, "tensor", axis=0, tiled=True)


def sum_grad(term_fn, row_count):
    return lax.psum_scatter(
        term_fn(jnp.int32(0), lax.axis_size("tensor") * row_count),
        "tensor",
        scatter_dimension=0,
        tiled=True,
    )


def normalize(total, gain, shift):
    row_mean = jnp.mean(total, axis=-1, keepdims=True)
    centered = total - row_mean
    spread = jnp.mean(centered * centered, axis=-1, keepdims=True)
    recip = lax.rsqrt(spread + EPSILON)
    normal = centered * recip
    return (normal * gain + shift, normal, recip)


def normalize_back(grad_in, normal, recip, gain):
    scaled = grad_in * gain
    inner = (
        scaled
        - jnp.mean(scaled, axis=-1, keepdims=True)
        - normal * jnp.mean(scaled * normal, axis=-1, keepdims=True)
    )
    return (recip * inner, jnp.sum(grad_in * normal, axis=0), jnp.sum(grad_in, axis=0))


def probabilities(query_block, keys_seq, first_row, prefix_len):
    block_rows = query_block.shape[0]
    scale = 1.0 / math.sqrt(HDIM)
    scores = (
        jnp.einsum("bhd,khd->hbk", query_block, keys_seq, preferred_element_type=jnp.float32)
        * scale
    )
    row_pos = first_row + lax.broadcasted_iota(jnp.int32, (block_rows, LEN), 0)
    col_pos = lax.broadcasted_iota(jnp.int32, (block_rows, LEN), 1)
    visible = (
        (col_pos <= row_pos) | (col_pos < prefix_len) | (row_pos < MEM) | (row_pos >= LEN - MEM)
    )
    scores = jnp.where(visible[None], scores, -1e30)
    row_max = jnp.max(scores, axis=-1, keepdims=True)
    expo = jnp.exp(scores - row_max)
    return expo / jnp.sum(expo, axis=-1, keepdims=True)


def attention_forward(query, keys, values, prefix):
    seq_count = prefix.shape[0]
    width = query.shape[1]
    local_heads = width // HDIM
    block_rows = min(512, LEN)
    block_count = LEN // block_rows
    shape_four = (seq_count, LEN, local_heads, HDIM)

    def per_sequence(sequence):
        query_seq, keys_seq, values_seq, prefix_len = sequence

        def per_block(block_index):
            first_row = block_index * block_rows
            query_block = lax.dynamic_slice_in_dim(query_seq, first_row, block_rows, 0)
            probs = probabilities(query_block, keys_seq, first_row, prefix_len)
            return jnp.einsum(
                "hbk,khd->bhd",
                probs.astype(jnp.bfloat16),
                values_seq,
                preferred_element_type=jnp.float32,
            ).astype(jnp.bfloat16)

        blocks = lax.map(per_block, jnp.arange(block_count, dtype=jnp.int32))
        return blocks.reshape(LEN, local_heads, HDIM)

    context = lax.map(
        per_sequence,
        (query.reshape(shape_four), keys.reshape(shape_four), values.reshape(shape_four), prefix),
    )
    return context.reshape(seq_count * LEN, width)


def attention_backward(query, keys, values, grad_context, prefix):
    seq_count = prefix.shape[0]
    width = query.shape[1]
    local_heads = width // HDIM
    block_rows = min(512, LEN)
    block_count = LEN // block_rows
    scale = 1.0 / math.sqrt(HDIM)
    shape_four = (seq_count, LEN, local_heads, HDIM)

    def per_sequence(sequence):
        query_seq, keys_seq, values_seq, grad_seq, prefix_len = sequence

        def per_block(running, block_index):
            keys_acc, values_acc = running
            first_row = block_index * block_rows
            query_block = lax.dynamic_slice_in_dim(query_seq, first_row, block_rows, 0)
            grad_block = lax.dynamic_slice_in_dim(grad_seq, first_row, block_rows, 0)
            probs = probabilities(query_block, keys_seq, first_row, prefix_len)
            probs_low = probs.astype(jnp.bfloat16)
            grad_probs = jnp.einsum(
                "bhd,khd->hbk",
                grad_block,
                values_seq,
                precision=HIGHEST,
                preferred_element_type=jnp.float32,
            )
            grad_scores = probs * (grad_probs - jnp.sum(probs * grad_probs, axis=-1, keepdims=True))
            grad_query = (
                jnp.einsum(
                    "hbk,khd->bhd",
                    grad_scores,
                    keys_seq,
                    precision=HIGHEST,
                    preferred_element_type=jnp.float32,
                )
                * scale
            )
            keys_acc = (
                keys_acc
                + jnp.einsum(
                    "hbk,bhd->khd",
                    grad_scores,
                    query_block,
                    precision=HIGHEST,
                    preferred_element_type=jnp.float32,
                )
                * scale
            )
            values_acc = values_acc + jnp.einsum(
                "hbk,bhd->khd",
                probs_low,
                grad_block,
                precision=HIGHEST,
                preferred_element_type=jnp.float32,
            )
            return ((keys_acc, values_acc), grad_query)

        zero_acc = jnp.zeros((LEN, local_heads, HDIM), jnp.float32)
        (keys_acc, values_acc), grad_query = lax.scan(
            per_block, (zero_acc, zero_acc), jnp.arange(block_count, dtype=jnp.int32)
        )
        return (grad_query.reshape(LEN, local_heads, HDIM), keys_acc, values_acc)

    grad_q, grad_k, grad_v = lax.map(
        per_sequence,
        (
            query.reshape(shape_four),
            keys.reshape(shape_four),
            values.reshape(shape_four),
            grad_context.reshape(shape_four),
            prefix,
        ),
    )
    flat = (seq_count * LEN, width)
    return (grad_q.reshape(flat), grad_k.reshape(flat), grad_v.reshape(flat))


def local(
    tokens,
    cotangent,
    prefix,
    w_qkv,
    bias_qv,
    w_out,
    bias_out,
    norm_gain,
    norm_bias,
    w_up,
    bias_up,
    w_down,
    bias_down,
):
    my_rows = tokens.shape[0]
    layer_count = w_qkv.shape[0]
    state = tokens.astype(jnp.float32)
    stored = []
    for layer_index in range(layer_count):
        input_whole = gather_rows(state.astype(jnp.bfloat16))
        query = (
            jnp.dot(input_whole, w_qkv[layer_index, 0], preferred_element_type=jnp.float32)
            + bias_qv[layer_index, 0]
        ).astype(jnp.bfloat16)
        keys = jnp.dot(
            input_whole, w_qkv[layer_index, 1], preferred_element_type=jnp.float32
        ).astype(jnp.bfloat16)
        values = (
            jnp.dot(input_whole, w_qkv[layer_index, 2], preferred_element_type=jnp.float32)
            + bias_qv[layer_index, 1]
        ).astype(jnp.bfloat16)
        context = attention_forward(query, keys, values, prefix)

        def attn_term(row_start, row_count):
            return jnp.dot(context, w_out[layer_index], preferred_element_type=jnp.float32)

        attn_share = sum_rows(attn_term, my_rows)
        normed, normal_one, recip_one = normalize(
            state + attn_share + bias_out[layer_index],
            norm_gain[layer_index, 0],
            norm_bias[layer_index, 0],
        )
        normed_whole = gather_rows(normed.astype(jnp.bfloat16))
        hidden = (
            jnp.dot(normed_whole, w_up[layer_index], preferred_element_type=jnp.float32)
            + bias_up[layer_index]
        )
        active = jax.nn.gelu(hidden, approximate=False).astype(jnp.bfloat16)

        def ffn_term(row_start, row_count):
            return jnp.dot(active, w_down[layer_index], preferred_element_type=jnp.float32)

        ffn_share = sum_rows(ffn_term, my_rows)
        state, normal_two, recip_two = normalize(
            normed + ffn_share + bias_down[layer_index],
            norm_gain[layer_index, 1],
            norm_bias[layer_index, 1],
        )
        stored.append(
            (
                input_whole,
                query,
                keys,
                values,
                context,
                normal_one,
                recip_one,
                normed_whole,
                hidden,
                active,
                normal_two,
                recip_two,
            )
        )
    grad_state = cotangent.astype(jnp.float32)
    weight_grads = [None] * layer_count
    bias_grads = [None] * layer_count
    shared_grads = [None] * layer_count
    for layer_index in reversed(range(layer_count)):
        (
            input_whole,
            query,
            keys,
            values,
            context,
            normal_one,
            recip_one,
            normed_whole,
            hidden,
            active,
            normal_two,
            recip_two,
        ) = stored[layer_index]
        grad_two, gain_two, shift_two = normalize_back(
            grad_state, normal_two, recip_two, norm_gain[layer_index, 1]
        )
        ffn_grad_whole = gather_grad(grad_two.astype(jnp.bfloat16))
        grad_down = jnp.einsum(
            "rf,rd->fd", active, ffn_grad_whole, preferred_element_type=jnp.float32
        )
        grad_active = jnp.einsum(
            "rd,fd->rf", ffn_grad_whole, w_down[layer_index], preferred_element_type=jnp.float32
        )
        _, gelu_pull = jax.vjp(functools.partial(jax.nn.gelu, approximate=False), hidden)
        grad_hidden = gelu_pull(grad_active)[0]
        grad_up = jnp.einsum(
            "rd,rf->df",
            normed_whole,
            grad_hidden,
            precision=HIGHEST,
            preferred_element_type=jnp.float32,
        )
        grad_bias_up = jnp.sum(grad_hidden, axis=0)

        def ffn_back_term(row_start, row_count):
            return jnp.einsum(
                "rf,df->rd",
                grad_hidden,
                w_up[layer_index],
                precision=HIGHEST,
                preferred_element_type=jnp.float32,
            )

        grad_normed = sum_grad(ffn_back_term, my_rows) + grad_two
        grad_one, gain_one, shift_one = normalize_back(
            grad_normed, normal_one, recip_one, norm_gain[layer_index, 0]
        )
        attn_grad_whole = gather_grad(grad_one.astype(jnp.bfloat16))
        grad_out = jnp.einsum(
            "rh,rd->hd", context, attn_grad_whole, preferred_element_type=jnp.float32
        )
        grad_context = jnp.einsum(
            "rd,hd->rh", attn_grad_whole, w_out[layer_index], preferred_element_type=jnp.float32
        )
        grad_query, grad_keys, grad_values = attention_backward(
            query, keys, values, grad_context, prefix
        )
        grad_qkv = jnp.stack(
            [
                jnp.einsum(
                    "rd,rh->dh",
                    input_whole,
                    grad_query,
                    precision=HIGHEST,
                    preferred_element_type=jnp.float32,
                ),
                jnp.einsum(
                    "rd,rh->dh",
                    input_whole,
                    grad_keys,
                    precision=HIGHEST,
                    preferred_element_type=jnp.float32,
                ),
                jnp.einsum(
                    "rd,rh->dh",
                    input_whole,
                    grad_values,
                    precision=HIGHEST,
                    preferred_element_type=jnp.float32,
                ),
            ]
        )
        grad_bias_qv = jnp.stack([jnp.sum(grad_query, axis=0), jnp.sum(grad_values, axis=0)])

        def input_back_term(row_start, row_count):
            total = jnp.einsum(
                "rh,dh->rd",
                grad_query,
                w_qkv[layer_index, 0],
                precision=HIGHEST,
                preferred_element_type=jnp.float32,
            )
            total = total + jnp.einsum(
                "rh,dh->rd",
                grad_keys,
                w_qkv[layer_index, 1],
                precision=HIGHEST,
                preferred_element_type=jnp.float32,
            )
            return total + jnp.einsum(
                "rh,dh->rd",
                grad_values,
                w_qkv[layer_index, 2],
                precision=HIGHEST,
                preferred_element_type=jnp.float32,
            )

        grad_state = sum_grad(input_back_term, my_rows) + grad_one
        weight_grads[layer_index] = (grad_qkv, grad_out, grad_up, grad_down)
        bias_grads[layer_index] = (grad_bias_qv, grad_bias_up)
        shared_grads[layer_index] = (
            jnp.sum(grad_one, axis=0),
            jnp.stack([gain_one, gain_two]),
            jnp.stack([shift_one, shift_two]),
            jnp.sum(grad_two, axis=0),
        )
    stacked_weights = tuple(
        (
            jnp.stack([weight_grads[level][member] for level in range(layer_count)])
            for member in range(4)
        )
    )
    summed_qkv, summed_out, summed_up, summed_down = (
        lax.psum_scatter(stacked_weights[0], "dp", scatter_dimension=2, tiled=True),
        lax.psum_scatter(stacked_weights[1], "dp", scatter_dimension=2, tiled=True),
        lax.psum_scatter(stacked_weights[2], "dp", scatter_dimension=1, tiled=True),
        lax.psum_scatter(stacked_weights[3], "dp", scatter_dimension=2, tiled=True),
    )
    stacked_bias_qv = jnp.stack([bias_grads[level][0] for level in range(layer_count)])
    stacked_bias_up = jnp.stack([bias_grads[level][1] for level in range(layer_count)])
    summed_bias_qv, summed_bias_up = lax.psum((stacked_bias_qv, stacked_bias_up), "dp")
    stacked_shared = tuple(
        (
            jnp.stack([shared_grads[level][member] for level in range(layer_count)])
            for member in range(4)
        )
    )
    summed_bias_out, summed_gain, summed_shift, summed_bias_down = lax.psum(
        stacked_shared, ("dp", "tensor")
    )
    return (
        state,
        grad_state,
        summed_qkv,
        summed_bias_qv,
        summed_out,
        summed_bias_out,
        summed_gain,
        summed_shift,
        summed_up,
        summed_bias_up,
        summed_down,
        summed_bias_down,
    )


def solution(mesh):
    in_specs = (
        P(("dp", "tensor"), None),
        P(("dp", "tensor"), None),
        P("dp"),
        P(None, None, None, "tensor"),
        P(None, None, "tensor"),
        P(None, "tensor", None),
        P(),
        P(),
        P(),
        P(None, None, "tensor"),
        P(None, "tensor"),
        P(None, "tensor", None),
        P(),
    )
    out_specs = (
        P(("dp", "tensor"), None),
        P(("dp", "tensor"), None),
        P(None, None, "dp", "tensor"),
        P(None, None, "tensor"),
        P(None, "tensor", "dp"),
        P(),
        P(),
        P(),
        P(None, "dp", "tensor"),
        P(None, "tensor"),
        P(None, "tensor", "dp"),
        P(),
    )
    return jax.shard_map(local, mesh=mesh, in_specs=in_specs, out_specs=out_specs, check_vma=False)
```

profile of v0, /device:TPU:0, one launch (start us, length us, event | category | flops | bytes accessed | tf_op | source)
XLA Modules:
  0.0 1125.7 jit_solution(9122916788855121678)
XLA Ops:
  8.7 23.2 %all-gather.9.cloned.1.call-done = bf16[1024,768]{1,0:T(8,128)(2,1)} async-done(((bf16[256,768]{1,0:T(8,128)(2,1)}), bf16[1024,768]{1,0:T(8,128)(2,1)}) %all-gather.9.cloned.1.call-update) | async-done | bytes 1572880 | tf_op jit(solution)/shard_map/all_gather | solution.py:16
  38.0 23.0 %while.86 = (s32[]{:T(128)}, bf16[2,512,3,64]{1,3,2,0:T(8,128)(2,1)S(1)}, s32[2]{0:T(128)S(1)}, s32[]{:T(128)}, bf16[1024,3,64]{0,2,1:T(8,128)(2,1)S(1)}, /*inde...) while((s32[]{:T(128)}, ...), condition=%wide.region_3.4_spmd, body=%wide.region_0.3_spmd.sunk | while | flops 414289920 | bytes 14833859 | solution.py:100
  40.6 5.0 fusion.388
  52.1 5.0 fusion.388
  65.6 37.9 %reduce-scatter.16.cloned.1.call-done = f32[256,768]{1,0:T(8,128)} async-done(((f32[1024,768]{1,0:T(8,128)}), f32[256,768]{1,0:T(8,128)}) %reduce-scatter.16.cloned.1.call-update) | async-done | bytes 786448 | tf_op jit(solution)/shard_map/reduce_scatter | solution.py:20
  106.6 19.2 %all-gather.11.cloned.1.call-done = bf16[1024,768]{1,0:T(8,128)(2,1)} async-done(((bf16[256,768]{1,0:T(8,128)(2,1)}), bf16[1024,768]{1,0:T(8,128)(2,1)}) %all-gather.11.cloned.1.call-update) | async-done | bytes 1572880 | tf_op jit(solution)/shard_map/all_gather | solution.py:16
  125.8 11.6 %multiply_convert_fusion.1 = (bf16[1024,768]{1,0:T(8,128)(2,1)S(1)}, f32[1024,768]{1,0:T(8,128)}, f32[1024,768]{1,0:T(8,128)}) fusion(f32[768]{0:T(1024)S(1)} %get-tuple-element.421, bf16[1024,768]{1,0:T(8,128)(2,1)} %all-gather.11.cloned.1.call-done, bf16[2,768,768]{2,1,0:T(8,128)(2,1)} %param.30), kind=kOutput, calls=%fused_computation.170 | convolution fusion | flops 1259864064 | bytes 10619904 | tf_op jit(solution)/shard_map/dot_general | solution.py:232
  142.4 37.4 %reduce-scatter.18.cloned.1.call-done = f32[256,768]{1,0:T(8,128)} async-done(((f32[1024,768]{1,0:T(8,128)}), f32[256,768]{1,0:T(8,128)}) %reduce-scatter.18.cloned.1.call-update) | async-done | bytes 786448 | tf_op jit(solution)/shard_map/reduce_scatter | solution.py:20
  182.6 19.8 %all-gather.13.cloned.1.call-done = bf16[1024,768]{1,0:T(8,128)(2,1)} async-done(((bf16[256,768]{1,0:T(8,128)(2,1)}), bf16[1024,768]{1,0:T(8,128)(2,1)}) %all-gather.13.cloned.1.call-update) | async-done | bytes 1572880 | tf_op jit(solution)/shard_map/all_gather | solution.py:16
  209.2 24.9 %while.87 = (s32[]{:T(128)}, bf16[2,512,3,64]{1,3,2,0:T(8,128)(2,1)S(1)}, s32[2]{0:T(128)S(1)}, s32[]{:T(128)}, bf16[1024,3,64]{0,2,1:T(8,128)(2,1)}, /*index=5*...) while((s32[]{:T(128)}, ...), condition=%wide.region_13.14_spmd, body=%wide.region_10.13_spmd.sunk | while | flops 414289920 | bytes 14833859 | solution.py:100
  211.7 5.9 fusion.395
  224.2 5.9 fusion.395
  237.8 37.8 %reduce-scatter.20.cloned.1.call-done = f32[256,768]{1,0:T(8,128)} async-done(((f32[1024,768]{1,0:T(8,128)}), f32[256,768]{1,0:T(8,128)}) %reduce-scatter.20.cloned.1.call-update) | async-done | bytes 786448 | tf_op jit(solution)/shard_map/reduce_scatter | solution.py:20
  278.4 19.8 %all-gather.15.cloned.1.call-done = bf16[1024,768]{1,0:T(8,128)(2,1)} async-done(((bf16[256,768]{1,0:T(8,128)(2,1)}), bf16[1024,768]{1,0:T(8,128)(2,1)}) %all-gather.15.cloned.1.call-update) | async-done | bytes 1572880 | tf_op jit(solution)/shard_map/all_gather | solution.py:16
  298.2 11.5 %multiply_convert_fusion = (bf16[1024,768]{1,0:T(8,128)(2,1)S(1)}, f32[1024,768]{1,0:T(8,128)}, f32[1024,768]{1,0:T(8,128)}) fusion(f32[768]{0:T(1024)S(1)} %get-tuple-element.420, bf16[1024,768]{1,0:T(8,128)(2,1)} %all-gather.15.cloned.1.call-done, bf16[2,768,768]{2,1,0:T(8,128)(2,1)} %param.30), kind=kOutput, calls=%fused_computation.157 | convolution fusion | flops 1259864064 | bytes 10619904 | tf_op jit(solution)/shard_map/dot_general | solution.py:232
  314.0 38.0 %reduce-scatter.22.cloned.1.call-done = f32[256,768]{1,0:T(8,128)} async-done(((f32[1024,768]{1,0:T(8,128)}), f32[256,768]{1,0:T(8,128)}) %reduce-scatter.22.cloned.1.call-update) | async-done | bytes 786448 | tf_op jit(solution)/shard_map/reduce_scatter | solution.py:20
  357.4 19.8 %all-gather.17.cloned.1.call-done = bf16[1024,768]{1,0:T(8,128)(2,1)} async-done(((bf16[256,768]{1,0:T(8,128)(2,1)}), bf16[1024,768]{1,0:T(8,128)(2,1)}) %all-gather.17.cloned.1.call-update) | async-done | bytes 1572880 | tf_op jit(solution)/shard_map/all_gather | solution.py:29
  377.2 6.5 fusion.279
  385.4 5.8 fusion.180
  391.3 38.1 %reduce-scatter.24.cloned.1.call-done = f32[256,768]{1,0:T(8,128)} async-done(((f32[1024,768]{1,0:T(8,128)}), f32[256,768]{1,0:T(8,128)}) %reduce-scatter.24.cloned.1.call-update) | async-done | bytes 786448 | tf_op jit(solution)/shard_map/reduce_scatter | solution.py:33
  435.2 18.8 %all-gather.19.cloned.1.call-done = bf16[1024,768]{1,0:T(8,128)(2,1)} async-done(((bf16[256,768]{1,0:T(8,128)(2,1)}), bf16[1024,768]{1,0:T(8,128)(2,1)}) %all-gather.19.cloned.1.call-update) | async-done | bytes 1572880 | tf_op jit(solution)/shard_map/all_gather | solution.py:29
  457.0 51.1 %while.88 = (s32[]{:T(128)}, f32[1024,3,64]{0,2,1:T(8,128)S(1)}, f32[1024,3,64]{0,2,1:T(8,128)S(1)}, f32[2,512,3,64]{1,3,2,0:T(8,128)S(1)}, s32[2]{0:T(128)S(1)}...) while((s32[]{:T(128)}, f32[1024,3,64]{0,2,1:T(8,128)S(1)}, ...), condition=%wide.region_29.30_spmd.clone, body=%wide.region_25.29_spmd.clone.sunk | while | flops 5059938816 | bytes 90376584 | solution.py:168
  459.6 6.1 fusion.406
  465.6 4.9 fusion.408
  477.8 4.5 fusion.409
  484.9 6.1 fusion.406
  491.0 4.9 fusion.408
  503.2 4.5 fusion.409
  518.0 38.0 %reduce-scatter.26.cloned.1.call-done = f32[256,768]{1,0:T(8,128)} async-done(((f32[1024,768]{1,0:T(8,128)}), f32[256,768]{1,0:T(8,128)}) %reduce-scatter.26.cloned.1.call-update) | async-done | bytes 786448 | tf_op jit(solution)/shard_map/reduce_scatter | solution.py:33
  560.1 19.6 %all-gather.21.cloned.1.call-done = bf16[1024,768]{1,0:T(8,128)(2,1)} async-done(((bf16[256,768]{1,0:T(8,128)(2,1)}), bf16[1024,768]{1,0:T(8,128)(2,1)}) %all-gather.21.cloned.1.call-update) | async-done | bytes 1572880 | tf_op jit(solution)/shard_map/all_gather | solution.py:29
  579.7 6.5 fusion.280
  587.9 5.8 fusion.190
  593.8 38.1 %reduce-scatter.28.cloned.1.call-done = f32[256,768]{1,0:T(8,128)} async-done(((f32[1024,768]{1,0:T(8,128)}), f32[256,768]{1,0:T(8,128)}) %reduce-scatter.28.cloned.1.call-update) | async-done | bytes 786448 | tf_op jit(solution)/shard_map/reduce_scatter | solution.py:33
  643.7 8.2 copy.37
  669.2 50.8 %while.89 = (s32[]{:T(128)}, f32[1024,3,64]{0,2,1:T(8,128)}, f32[1024,3,64]{0,2,1:T(8,128)S(1)}, f32[2,512,3,64]{1,3,2,0:T(8,128)S(1)}, s32[2]{0:T(128)S(1)}, /*...) while((s32[]{:T(128)}, f32[1024,3,64]{0,2,1:T(8,128)}, ...), condition=%wide.region_40.41_spmd.clone, body=%wide.region_36.40_spmd.clone.sunk | while | flops 5059938816 | bytes 95097240 | solution.py:168
  671.8 6.0 fusion.419
  677.8 4.9 fusion.421
  697.0 6.0 fusion.419
  703.0 4.9 fusion.421
  738.8 4.8 copy.40
  743.6 8.0 reshape.422
  753.7 5.6 convolution_bitcast_fusion.2
  768.5 61.6 %all-reduce.5.cloned.1.call-done = f32[2,768,768]{1,0,2:T(2,128)} async-done(((f32[2,768,768]{1,0,2:T(2,128)}), f32[2,768,768]{1,0,2:T(2,128)}) %all-reduce.5.cloned.1.call-update) | async-done | bytes 4718608
  832.2 40.7 %all-reduce.1 = (f32[2,768]{1,0:T(2,128)}, f32[2,2,768]{2,1,0:T(2,128)}, f32[2,2,768]{2,1,0:T(2,128)}, f32[2,768]{1,0:T(2,128)}) all-reduce(f32[2,768]{1,0:T(2,128)S(1)} %pad_maximum_fusion.6, f32[2,2,768]{2,1,0:T(2,128)S(1)} %pad_maximum_fusion.4, ...), channel_id=1, replica_groups=mesh['dp'=8,'tensor'=4] {'dp','tensor'}, use_global_device_ids=true, to_apply=%region_51.52 | all-reduce | flops 9216 | bytes 73728 | tf_op jit(solution)/shard_map/psum | solution.py:405
  873.3 36.8 %all-reduce.2 = (f32[2,2,192]{2,1,0:T(2,128)}, f32[2,768]{1,0:T(2,128)}) all-reduce(f32[2,2,192]{2,1,0:T(2,128)S(1)} %pad_maximum_fusion.9, f32[2,768]{1,0:T(2,128)S(1)} %pad_maximum_fusion.7), channel_id=1, replica_groups=mesh['dp'=8,'tensor'=4] {'dp'}, use_global_device_ids=true, to_apply=%region_47.48 | all-reduce | flops 2304 | bytes 18432 | tf_op jit(solution)/shard_map/psum | solution.py:398
  912.0 24.5 %reduce-scatter.30.cloned.1.call-done = f32[256,768]{1,0:T(8,128)} async-done(((f32[1024,768]{1,0:T(8,128)}), f32[256,768]{1,0:T(8,128)}) %reduce-scatter.30.cloned.1.call-update) | async-done | bytes 786448 | tf_op jit(solution)/shard_map/reduce_scatter | solution.py:33
  938.7 80.7 %reduce-scatter.34.cloned.1.call-done = f32[96,1152]{1,0:T(8,128)} async-done(((f32[768,1152]{1,0:T(8,128)}), f32[96,1152]{1,0:T(8,128)}) %reduce-scatter.34.cloned.1.call-update) | async-done | bytes 442384
  1021.9 96.7 %reduce-scatter.32.cloned.1.call-done = f32[2,96,768]{2,1,0:T(8,128)} async-done(((f32[2,768,768]{2,1,0:T(8,128)}), f32[2,96,768]{2,1,0:T(8,128)}) %reduce-scatter.32.cloned.1.call-update) | async-done | bytes 589840 | tf_op jit(solution)/shard_map/reduce_scatter | solution.py:393
  (472 shorter events, 206.8 us)
Async XLA Ops:
  7.2 24.8 %all-gather.9.cloned.1.call-start = ((), (), s32[]{:S(2)}) async-start(), calls=%async_computation.11 | async-start | bytes 1966080 | tf_op jit(solution)/shard_map/all_gather | solution.py:16
  7.9 95.5 %reduce-scatter.16.cloned.1.call-start = ((), (), s32[]{:S(2)}) async-start(), calls=%async_computation.12 | async-start | bytes 3932160 | tf_op jit(solution)/shard_map/reduce_scatter | solution.py:20
  63.0 40.4 %copy-start.46 = (bf16[256,768]{1,0:T(8,128)(2,1)S(1)}, bf16[256,768]{1,0:T(8,128)(2,1)}, u32[]{:S(2)}) copy-start(bf16[256,768]{1,0:T(8,128)(2,1)} %param.21) | copy-start | bytes 1179652
  65.3 41.2 %copy-start.77 = (f32[2,768]{1,0:T(2,128)S(1)}, f32[2,768]{1,0:T(2,128)}, u32[]{:S(2)}) copy-start(f32[2,768]{1,0:T(2,128)} %param.31) | copy-start | bytes 18436
  65.4 60.4 %all-gather.11.cloned.1.call-start = ((), (), s32[]{:S(2)}) async-start(), calls=%async_computation.13 | async-start | bytes 1966080 | tf_op jit(solution)/shard_map/all_gather | solution.py:16
  65.5 114.3 %copy-start.50 = (f32[768]{0:T(1024)}, f32[768]{0:T(1024)S(1)}, u32[]{:S(2)}) copy-start(f32[768]{0:T(1024)S(1)} %get-tuple-element.555) | copy-start | bytes 9220
  65.6 210.1 %copy-start.52 = (f32[768]{0:T(1024)}, f32[768]{0:T(1024)S(1)}, u32[]{:S(2)}) copy-start(f32[768]{0:T(1024)S(1)} %get-tuple-element.556) | copy-start | bytes 9220
  104.8 75.1 %copy-start = (f32[256,768]{1,0:T(8,128)}, f32[256,768]{1,0:T(8,128)S(1)}, u32[]{:S(2)}) copy-start(f32[256,768]{1,0:T(8,128)S(1)} %get-tuple-element.520) | copy-start | bytes 2359300
  104.8 75.1 %copy-start.54 = (f32[256]{0:T(256)}, f32[256]{0:T(256)S(1)}, u32[]{:S(2)}) copy-start(f32[256]{0:T(256)S(1)} %broadcast_multiply_fusion.11) | copy-start | bytes 3076
  105.0 74.8 %copy-start.58 = (f32[256]{0:T(256)}, f32[256]{0:T(256)S(1)}, u32[]{:S(2)}) copy-start(f32[256]{0:T(256)S(1)} %add_rsqrt_fusion.3) | copy-start | bytes 3076
  106.0 73.9 %reduce-scatter.18.cloned.1.call-start = ((), (), s32[]{:S(2)}) async-start(), calls=%async_computation.14 | async-start | bytes 3932160 | tf_op jit(solution)/shard_map/reduce_scatter | solution.py:20
  141.7 60.7 %all-gather.13.cloned.1.call-start = ((), (), s32[]{:S(2)}) async-start(), calls=%async_computation.15 | async-start | bytes 1966080 | tf_op jit(solution)/shard_map/all_gather | solution.py:16
  181.3 94.3 %copy-start.2 = (f32[256,768]{1,0:T(8,128)}, f32[256,768]{1,0:T(8,128)S(1)}, u32[]{:S(2)}) copy-start(f32[256,768]{1,0:T(8,128)S(1)} %get-tuple-element.516) | copy-start | bytes 2359300
  181.4 94.3 %copy-start.56 = (f32[256]{0:T(256)}, f32[256]{0:T(256)S(1)}, u32[]{:S(2)}) copy-start(f32[256]{0:T(256)S(1)} %broadcast_multiply_fusion.10) | copy-start | bytes 3076
  181.6 94.1 %copy-start.60 = (f32[256]{0:T(256)}, f32[256]{0:T(256)S(1)}, u32[]{:S(2)}) copy-start(f32[256]{0:T(256)S(1)} %add_rsqrt_fusion.2) | copy-start | bytes 3076
  182.6 93.1 %reduce-scatter.20.cloned.1.call-start = ((), (), s32[]{:S(2)}) async-start(), calls=%async_computation.16 | async-start | bytes 3932160 | tf_op jit(solution)/shard_map/reduce_scatter | solution.py:20
  237.6 60.6 %all-gather.15.cloned.1.call-start = ((), (), s32[]{:S(2)}) async-start(), calls=%async_computation.17 | async-start | bytes 1966080 | tf_op jit(solution)/shard_map/all_gather | solution.py:16
  278.4 73.7 %reduce-scatter.22.cloned.1.call-start = ((), (), s32[]{:S(2)}) async-start(), calls=%async_computation.18 | async-start | bytes 3932160 | tf_op jit(solution)/shard_map/reduce_scatter | solution.py:20
  313.9 39.8 %copy-start.47 = (bf16[256,768]{1,0:T(8,128)(2,1)S(1)}, bf16[256,768]{1,0:T(8,128)(2,1)}, u32[]{:S(2)}) copy-start(bf16[256,768]{1,0:T(8,128)(2,1)} %param.22) | copy-start | bytes 1179652
  314.0 63.2 %all-gather.17.cloned.1.call-start = ((), (), s32[]{:S(2)}) async-start(), calls=%async_computation.19 | async-start | bytes 1966080 | tf_op jit(solution)/shard_map/all_gather | solution.py:29
  357.4 72.0 %reduce-scatter.24.cloned.1.call-start = ((), (), s32[]{:S(2)}) async-start(), calls=%async_computation.20 | async-start | bytes 3932160 | tf_op jit(solution)/shard_map/reduce_scatter | solution.py:33
  391.2 62.7 %all-gather.19.cloned.1.call-start = ((), (), s32[]{:S(2)}) async-start(), calls=%async_computation.21 | async-start | bytes 1966080 | tf_op jit(solution)/shard_map/all_gather | solution.py:29
  434.1 121.9 %reduce-scatter.26.cloned.1.call-start = ((), (), s32[]{:S(2)}) async-start(), calls=%async_computation.22 | async-start | bytes 3932160 | tf_op jit(solution)/shard_map/reduce_scatter | solution.py:33
  517.9 38.1 %copy-start.3 = (f32[256,768]{1,0:T(8,128)S(1)}, f32[256,768]{1,0:T(8,128)}, u32[]{:S(2)}) copy-start(f32[256,768]{1,0:T(8,128)} %copy-done.2) | copy-start | bytes 2359300
  517.9 38.1 %copy-start.23 = (f32[256,768]{1,0:T(8,128)S(1)}, f32[256,768]{1,0:T(8,128)}, u32[]{:S(2)}) copy-start(f32[256,768]{1,0:T(8,128)} %copy-done.22) | copy-start | bytes 2359300
  517.9 38.1 %copy-start.53 = (f32[768]{0:T(1024)S(1)}, f32[768]{0:T(1024)}, u32[]{:S(2)}) copy-start(f32[768]{0:T(1024)} %copy-done.52) | copy-start | bytes 9220
  517.9 38.1 %copy-start.57 = (f32[256]{0:T(256)S(1)}, f32[256]{0:T(256)}, u32[]{:S(2)}) copy-start(f32[256]{0:T(256)} %copy-done.56) | copy-start | bytes 3076
  517.9 38.1 %copy-start.61 = (f32[256]{0:T(256)S(1)}, f32[256]{0:T(256)}, u32[]{:S(2)}) copy-start(f32[256]{0:T(256)} %copy-done.60) | copy-start | bytes 3076
  517.9 61.8 %copy-start.80 = (f32[768]{0:T(1024)S(1)}, f32[768]{0:T(1024)}, u32[]{:S(2)}) copy-start(f32[768]{0:T(1024)} %copy-done.79) | copy-start | bytes 9220
  517.9 61.8 %all-gather.21.cloned.1.call-start = ((), (), s32[]{:S(2)}) async-start(), calls=%async_computation.23 | async-start | bytes 1966080 | tf_op jit(solution)/shard_map/all_gather | solution.py:29
  559.9 72.0 %reduce-scatter.28.cloned.1.call-start = ((), (), s32[]{:S(2)}) async-start(), calls=%async_computation.24 | async-start | bytes 3932160 | tf_op jit(solution)/shard_map/reduce_scatter | solution.py:33
  593.7 38.2 %copy-start.1 = (f32[256,768]{1,0:T(8,128)S(1)}, f32[256,768]{1,0:T(8,128)}, u32[]{:S(2)}) copy-start(f32[256,768]{1,0:T(8,128)} %copy-done) | copy-start | bytes 2359300
  593.7 38.2 %copy-start.51 = (f32[768]{0:T(1024)S(1)}, f32[768]{0:T(1024)}, u32[]{:S(2)}) copy-start(f32[768]{0:T(1024)} %copy-done.50) | copy-start | bytes 9220
  593.7 38.2 %copy-start.55 = (f32[256]{0:T(256)S(1)}, f32[256]{0:T(256)}, u32[]{:S(2)}) copy-start(f32[256]{0:T(256)} %copy-done.54) | copy-start | bytes 3076
  593.7 38.2 %copy-start.59 = (f32[256]{0:T(256)S(1)}, f32[256]{0:T(256)}, u32[]{:S(2)}) copy-start(f32[256]{0:T(256)} %copy-done.58) | copy-start | bytes 3076
  593.8 43.0 %copy-start.86 = (bf16[1024,768]{1,0:T(8,128)(2,1)S(1)}, bf16[1024,768]{1,0:T(8,128)(2,1)}, u32[]{:S(2)}) copy-start(bf16[1024,768]{1,0:T(8,128)(2,1)} %all-gather.17.cloned.1.call-done) | copy-start | bytes 4718596
  593.8 62.7 %all-gather.23.cloned.1.call-start = ((), (), s32[]{:S(2)}) async-start(), calls=%async_computation.25 | async-start | bytes 1966080 | tf_op jit(solution)/shard_map/all_gather | solution.py:29
  636.7 193.4 %all-reduce.5.cloned.1.call-start = ((), (), s32[]{:S(2)}) async-start(), calls=%async_computation.30 | async-start | bytes 9437184
  651.9 258.2 %reduce-scatter.36.cloned.1.call-start = ((), (), s32[]{:S(2)}) async-start(), calls=%async_computation.29 | async-start | bytes 1327104
  667.4 269.2 %reduce-scatter.30.cloned.1.call-start = ((), (), s32[]{:S(2)}) async-start(), calls=%async_computation.26 | async-start | bytes 3932160 | tf_op jit(solution)/shard_map/reduce_scatter | solution.py:33
  729.5 289.8 %reduce-scatter.34.cloned.1.call-start = ((), (), s32[]{:S(2)}) async-start(), calls=%async_computation.28 | async-start | bytes 3981312
  751.6 367.0 %reduce-scatter.32.cloned.1.call-start = ((), (), s32[]{:S(2)}) async-start(), calls=%async_computation.27 | async-start | bytes 5308416 | tf_op jit(solution)/shard_map/reduce_scatter | solution.py:393
  766.0 66.1 %copy-start.72 = (f32[768]{0:T(1024)S(1)}, f32[768]{0:T(1024)}, u32[]{:S(2)}) copy-start(f32[768]{0:T(1024)} %get-tuple-element.394) | copy-start | bytes 9220
  766.0 66.1 %copy-start.73 = (f32[768]{0:T(1024)S(1)}, f32[768]{0:T(1024)}, u32[]{:S(2)}) copy-start(f32[768]{0:T(1024)} %get-tuple-element.502) | copy-start | bytes 9220
  766.0 66.1 %copy-start.71 = (f32[768]{0:T(1024)S(1)}, f32[768]{0:T(1024)}, u32[]{:S(2)}) copy-start(f32[768]{0:T(1024)} %get-tuple-element.405) | copy-start | bytes 9220
  766.0 106.9 %copy-start.19 = (f32[2,512,3,64]{1,3,2,0:T(8,128)S(1)}, f32[2,512,3,64]{1,3,2,0:T(8,128)}, u32[]{:S(2)}) copy-start(f32[2,512,3,64]{1,3,2,0:T(8,128)} %copy-done.18) | copy-start | bytes 2359300
  766.0 107.1 %copy-start.12 = (f32[1024,3,64]{0,2,1:T(8,128)S(1)}, f32[1024,3,64]{0,2,1:T(8,128)}, u32[]{:S(2)}) copy-start(f32[1024,3,64]{0,2,1:T(8,128)} %copy-done.10) | copy-start | bytes 2359300
  768.0 168.5 %copy-start.21 = (f32[256,768]{1,0:T(8,128)S(1)}, f32[256,768]{1,0:T(8,128)}, u32[]{:S(2)}) copy-start(f32[256,768]{1,0:T(8,128)} %copy-done.20) | copy-start | bytes 2359300
  (88 other events, 356.8 us)
Sparse Core Ops, SparseCore 0:
  9.6 22.3 all-gather.8
  65.5 37.9 reduce-scatter.15
  106.1 19.6 all-gather.10
  141.9 37.9 reduce-scatter.17
  182.7 19.6 all-gather.12
  237.7 37.9 reduce-scatter.19
  278.5 19.6 all-gather.14
  314.1 37.9 reduce-scatter.21
  357.5 19.6 all-gather.16
  391.4 37.9 reduce-scatter.23
  434.2 19.6 all-gather.18
  518.0 37.9 reduce-scatter.25
  560.0 19.6 all-gather.20
  593.9 37.9 reduce-scatter.27
  636.8 19.6 all-gather.22
  660.4 169.6 all-reduce.4
  833.7 63.2 reduce-scatter.35
  899.5 36.9 reduce-scatter.29
  940.2 79.0 reduce-scatter.33
  1023.4 95.1 reduce-scatter.31
where the time goes:
time: 1130 us
  waiting for transfers between devices  672 us (59%)
  matrix products  242 us (21%)
  blocking collectives  77.5 us (7%)
  local copies, waits for them, and re-layouts  63.6 us (6%)
  other arithmetic  45.1 us (4%)
  between operations  16.6 us (1%)
    reduce_scatter x4, waiting for transfers between devices, sum_rows(): lax.psum_scatter(term_fn(jnp.int32(0), lax.axis_size('tensor') * row_coun...  151 us
    unnamed x23, waiting for transfers between devices  143 us
    reduce_scatter x4, waiting for transfers between devices, sum_grad(): lax.psum_scatter(term_fn(jnp.int32(0), lax.axis_size('tensor') * row_coun...  139 us
    reduce_scatter x1, waiting for transfers between devices, local(): lax.psum_scatter(stacked_weights[2], 'dp', scatter_dimension=1, tiled=True)  96.7 us
    all_gather x4, waiting for transfers between devices, gather_rows(): return lax.all_gather(values_in, 'tensor', axis=0, tiled=True)  82 us
    all_gather x4, waiting for transfers between devices, gather_grad(): return lax.all_gather(values_in, 'tensor', axis=0, tiled=True)  60 us
    unnamed x203, local copies, waits for them, and re-layouts  46.1 us
    sub x8, matrix products, probabilities(): expo = jnp.exp(scores - row_max)  45.9 us
  transfers between devices with their start and end apart: 20, of which 19 were waited for; matrix products, arithmetic and copies ran while one was open for 12% of the time, Pallas kernels for 0%

commit v1 on v0

--- a/solution.py
+++ b/solution.py
@@ -12,8 +12,20 @@
 HIGHEST = lax.Precision.HIGHEST
 
 
+def gather_by_bits(x, axis, dim):
+    ways, here, step = (lax.axis_size(axis), lax.axis_index(axis), x.shape[dim])
+    line, have = (x, 1)
+    while have < ways:
+        line = jnp.concatenate(
+            [line, lax.ppermute(line, axis, [(d, (d - have) % ways) for d in range(ways)])],
+            axis=dim,
+        )
+        have = 2 * have
+    return jnp.roll(line, here * step, axis=dim)
+
+
 def gather_rows(values_in):
-    return lax.all_gather(values_in, "tensor", axis=0, tiled=True)
+    return gather_by_bits(values_in, "tensor", 0)
 
 
 def sum_rows(term_fn, row_count):

time: 1130 us -> 1170 us (1.035)
  waiting for transfers between devices: 672 us -> 691 us
  other arithmetic: 45.1 us -> 63.6 us
    ppermute x0 -> x8, waiting for transfers between devices: none -> 95.2 us  [gather_by_bits(): lax.ppermute(line, axis, [(d, (d - have) % ways) for d in range(ways)])]
    all_gather x4 -> x0, waiting for transfers between devices: 82 us -> none  [gather_rows(): return lax.all_gather(values_in, 'tensor', axis=0, tiled=True)]
    concatenate x0 -> x8, other arithmetic: none -> 21.8 us  [the longest x4 20.6 us: gather_by_bits(): return jnp.roll(line, here * step, axis=dim)]
    unnamed x203 -> x211, local copies, waits for them, and re-layouts: 46.1 us -> 43.8 us
    unnamed x23 -> x19, waiting for transfers between devices: 143 us -> 144 us
  transfers between devices with their start and end apart: 20 -> 24, of which waited for: 19 -> 23; matrix products, arithmetic and copies ran while one was open for 12% -> 11% of each run, Pallas kernels for 0% -> 0%
where the time goes in v1:
time: 1170 us; the launch traced here: 1160 us
  waiting for transfers between devices  691 us (59%)
  matrix products  235 us (20%)
  blocking collectives  77.5 us (7%)
  other arithmetic  63.6 us (5%)
  local copies, waits for them, and re-layouts  61.6 us (5%)
  between operations  16.4 us (1%)
    reduce_scatter x4, waiting for transfers between devices, sum_rows(): lax.psum_scatter(term_fn(jnp.int32(0), lax.axis_size('tensor') * row_coun...  156 us
    unnamed x19, waiting for transfers between devices  144 us
    reduce_scatter x4, waiting for transfers between devices, sum_grad(): lax.psum_scatter(term_fn(jnp.int32(0), lax.axis_size('tensor') * row_coun...  139 us
    reduce_scatter x1, waiting for transfers between devices, local(): lax.psum_scatter(stacked_weights[2], 'dp', scatter_dimension=1, tiled=True)  96.8 us
    ppermute x8, waiting for transfers between devices, gather_by_bits(): lax.ppermute(line, axis, [(d, (d - have) % ways) for d in range(ways)])  95.2 us
    all_gather x4, waiting for transfers between devices, gather_grad(): return lax.all_gather(values_in, 'tensor', axis=0, tiled=True)  59.5 us
    sub x8, matrix products, probabilities(): expo = jnp.exp(scores - row_max)  47.9 us
    unnamed x211, local copies, waits for them, and re-layouts  43.8 us
  transfers between devices with their start and end apart: 24, of which 23 were waited for; matrix products, arithmetic and copies ran while one was open for 11% of the time, Pallas kernels for 0%

profile of v1, /device:TPU:0, one launch (start us, length us, event | category | flops | bytes accessed | tf_op | source)
XLA Modules:
  0.0 1162.1 jit_solution(8466695938273648285)
XLA Ops:
  9.7 5.6 collective-permute-done
  17.8 19.0 %collective-permute-done.1 = bf16[512,768]{1,0:T(8,128)(2,1)} collective-permute-done((bf16[512,768]{1,0:T(8,128)(2,1)S(1)}, bf16[512,768]{1,0:T(8,128)(2,1)}, u32[]{:S(2)}, u32[]{:S(2)}) %collective-permute-start.1) | collective-permute-done | bytes 786464 | tf_op jit(solution)/shard_map/ppermute | solution.py:20
  44.3 24.8 %while.86 = (s32[]{:T(128)}, bf16[2,512,3,64]{1,3,2,0:T(8,128)(2,1)S(1)}, s32[2]{0:T(128)S(1)}, s32[]{:T(128)}, bf16[1024,3,64]{0,2,1:T(8,128)(2,1)}, /*index=5*...) while((s32[]{:T(128)}, ...), condition=%wide.region_3.5_spmd, body=%wide.region_0.4_spmd.sunk | while | flops 414289920 | bytes 14833859 | solution.py:112
  46.9 5.9 fusion.408
  59.3 5.9 fusion.408
  72.9 38.2 %reduce-scatter.16.cloned.1.call-done = f32[256,768]{1,0:T(8,128)} async-done(((f32[1024,768]{1,0:T(8,128)}), f32[256,768]{1,0:T(8,128)}) %reduce-scatter.16.cloned.1.call-update) | async-done | bytes 786448 | tf_op jit(solution)/shard_map/reduce_scatter | solution.py:32
  113.2 5.3 collective-permute-done.2
  120.1 18.2 %collective-permute-done.3 = bf16[512,768]{1,0:T(8,128)(2,1)S(1)} collective-permute-done((bf16[512,768]{1,0:T(8,128)(2,1)S(1)}, bf16[512,768]{1,0:T(8,128)(2,1)S(1)}, u32[]{:S(2)}, u32[]{:S(2)}) %collective-permute-start.3) | collective-permute-done | bytes 786464 | tf_op jit(solution)/shard_map/ppermute | solution.py:20
  138.3 5.3 fusion.178
  143.6 9.2 multiply_convert_fusion.1
  157.8 38.9 %reduce-scatter.18.cloned.1.call-done = f32[256,768]{1,0:T(8,128)} async-done(((f32[1024,768]{1,0:T(8,128)}), f32[256,768]{1,0:T(8,128)}) %reduce-scatter.18.cloned.1.call-update) | async-done | bytes 786448 | tf_op jit(solution)/shard_map/reduce_scatter | solution.py:32
  199.0 5.3 collective-permute-done.4
  205.8 18.4 %collective-permute-done.5 = bf16[512,768]{1,0:T(8,128)(2,1)} collective-permute-done((bf16[512,768]{1,0:T(8,128)(2,1)S(1)}, bf16[512,768]{1,0:T(8,128)(2,1)}, u32[]{:S(2)}, u32[]{:S(2)}) %collective-permute-start.5) | collective-permute-done | bytes 786464 | tf_op jit(solution)/shard_map/ppermute | solution.py:20
  224.2 5.3 fusion.173
  235.4 24.9 %while.87 = (s32[]{:T(128)}, bf16[2,512,3,64]{1,3,2,0:T(8,128)(2,1)S(1)}, s32[2]{0:T(128)S(1)}, s32[]{:T(128)}, bf16[1024,3,64]{0,2,1:T(8,128)(2,1)}, /*index=5*...) while((s32[]{:T(128)}, ...), condition=%wide.region_13.15_spmd, body=%wide.region_10.14_spmd.sunk | while | flops 414289920 | bytes 14833859 | solution.py:112
  238.0 5.9 fusion.415
  250.4 5.9 fusion.415
  263.9 39.5 %reduce-scatter.20.cloned.1.call-done = f32[256,768]{1,0:T(8,128)} async-done(((f32[1024,768]{1,0:T(8,128)}), f32[256,768]{1,0:T(8,128)}) %reduce-scatter.20.cloned.1.call-update) | async-done | bytes 786448 | tf_op jit(solution)/shard_map/reduce_scatter | solution.py:32
  305.8 5.3 collective-permute-done.6
  312.7 18.2 %collective-permute-done.7 = bf16[512,768]{1,0:T(8,128)(2,1)S(1)} collective-permute-done((bf16[512,768]{1,0:T(8,128)(2,1)S(1)}, bf16[512,768]{1,0:T(8,128)(2,1)S(1)}, u32[]{:S(2)}, u32[]{:S(2)}) %collective-permute-start.7) | collective-permute-done | bytes 786464 | tf_op jit(solution)/shard_map/ppermute | solution.py:20
  330.9 5.3 fusion.168
  336.2 9.2 multiply_convert_fusion
  349.7 39.6 %reduce-scatter.22.cloned.1.call-done = f32[256,768]{1,0:T(8,128)} async-done(((f32[1024,768]{1,0:T(8,128)}), f32[256,768]{1,0:T(8,128)}) %reduce-scatter.22.cloned.1.call-update) | async-done | bytes 786448 | tf_op jit(solution)/shard_map/reduce_scatter | solution.py:32
  394.8 19.6 %all-gather.5.cloned.1.call-done = bf16[1024,768]{1,0:T(8,128)(2,1)} async-done(((bf16[256,768]{1,0:T(8,128)(2,1)}), bf16[1024,768]{1,0:T(8,128)(2,1)}) %all-gather.5.cloned.1.call-update) | async-done | bytes 1572880 | tf_op jit(solution)/shard_map/all_gather | solution.py:41
  414.4 6.5 fusion.299
  422.6 5.8 fusion.200
  428.5 38.1 %reduce-scatter.24.cloned.1.call-done = f32[256,768]{1,0:T(8,128)} async-done(((f32[1024,768]{1,0:T(8,128)}), f32[256,768]{1,0:T(8,128)}) %reduce-scatter.24.cloned.1.call-update) | async-done | bytes 786448 | tf_op jit(solution)/shard_map/reduce_scatter | solution.py:45
  472.4 18.8 %all-gather.7.cloned.1.call-done = bf16[1024,768]{1,0:T(8,128)(2,1)} async-done(((bf16[256,768]{1,0:T(8,128)(2,1)}), bf16[1024,768]{1,0:T(8,128)(2,1)}) %all-gather.7.cloned.1.call-update) | async-done | bytes 1572880 | tf_op jit(solution)/shard_map/all_gather | solution.py:41
  494.2 50.8 %while.88 = (s32[]{:T(128)}, f32[1024,3,64]{0,2,1:T(8,128)S(1)}, f32[1024,3,64]{0,2,1:T(8,128)S(1)}, f32[2,512,3,64]{1,3,2,0:T(8,128)S(1)}, s32[2]{0:T(128)S(1)}...) while((s32[]{:T(128)}, f32[1024,3,64]{0,2,1:T(8,128)S(1)}, ...), condition=%wide.region_29.31_spmd.clone, body=%wide.region_25.30_spmd.clone.sunk | while | flops 5059938816 | bytes 90376584 | solution.py:180
  496.7 6.1 fusion.426
  522.0 6.1 fusion.426
  554.9 38.0 %reduce-scatter.26.cloned.1.call-done = f32[256,768]{1,0:T(8,128)} async-done(((f32[1024,768]{1,0:T(8,128)}), f32[256,768]{1,0:T(8,128)}) %reduce-scatter.26.cloned.1.call-update) | async-done | bytes 786448 | tf_op jit(solution)/shard_map/reduce_scatter | solution.py:45
  597.3 19.3 %all-gather.9.cloned.1.call-done = bf16[1024,768]{1,0:T(8,128)(2,1)} async-done(((bf16[256,768]{1,0:T(8,128)(2,1)}), bf16[1024,768]{1,0:T(8,128)(2,1)}) %all-gather.9.cloned.1.call-update) | async-done | bytes 1572880 | tf_op jit(solution)/shard_map/all_gather | solution.py:41
  616.6 6.5 fusion.300
  624.8 5.8 fusion.210
  630.7 38.1 %reduce-scatter.28.cloned.1.call-done = f32[256,768]{1,0:T(8,128)} async-done(((f32[1024,768]{1,0:T(8,128)}), f32[256,768]{1,0:T(8,128)}) %reduce-scatter.28.cloned.1.call-update) | async-done | bytes 786448 | tf_op jit(solution)/shard_map/reduce_scatter | solution.py:45
  680.6 8.2 copy.37
  703.7 51.1 %while.89 = (s32[]{:T(128)}, f32[1024,3,64]{0,2,1:T(8,128)S(1)}, f32[1024,3,64]{0,2,1:T(8,128)S(1)}, f32[2,512,3,64]{1,3,2,0:T(8,128)S(1)}, s32[2]{0:T(128)S(1)}...) while((s32[]{:T(128)}, f32[1024,3,64]{0,2,1:T(8,128)S(1)}, ...), condition=%wide.region_40.42_spmd.clone, body=%wide.region_36.41_spmd.clone.sunk | while | flops 5059938816 | bytes 90376584 | solution.py:180
  706.3 6.1 fusion.439
  731.7 6.1 fusion.439
  778.3 8.0 reshape.422
  788.3 5.7 convolution_bitcast_fusion.2
  803.2 63.7 %all-reduce.5.cloned.1.call-done = f32[2,768,768]{1,0,2:T(2,128)} async-done(((f32[2,768,768]{1,0,2:T(2,128)}), f32[2,768,768]{1,0,2:T(2,128)}) %all-reduce.5.cloned.1.call-update) | async-done | bytes 4718608
  869.0 40.8 %all-reduce.1 = (f32[2,768]{1,0:T(2,128)}, f32[2,2,768]{2,1,0:T(2,128)}, f32[2,2,768]{2,1,0:T(2,128)}, f32[2,768]{1,0:T(2,128)}) all-reduce(f32[2,768]{1,0:T(2,128)S(1)} %pad_maximum_fusion.10, f32[2,2,768]{2,1,0:T(2,128)S(1)} %pad_maximum_fusion.8, ...), channel_id=1, replica_groups=mesh['dp'=8,'tensor'=4] {'dp','tensor'}, use_global_device_ids=true, to_apply=%region_51.53 | all-reduce | flops 9216 | bytes 73728 | tf_op jit(solution)/shard_map/psum | solution.py:417
  910.3 36.8 %all-reduce.2 = (f32[2,2,192]{2,1,0:T(2,128)}, f32[2,768]{1,0:T(2,128)}) all-reduce(f32[2,2,192]{2,1,0:T(2,128)S(1)} %pad_maximum_fusion.13, f32[2,768]{1,0:T(2,128)S(1)} %pad_maximum_fusion.11), channel_id=1, replica_groups=mesh['dp'=8,'tensor'=4] {'dp'}, use_global_device_ids=true, to_apply=%region_47.49 | all-reduce | flops 2304 | bytes 18432 | tf_op jit(solution)/shard_map/psum | solution.py:410
  948.9 24.6 %reduce-scatter.30.cloned.1.call-done = f32[256,768]{1,0:T(8,128)} async-done(((f32[1024,768]{1,0:T(8,128)}), f32[256,768]{1,0:T(8,128)}) %reduce-scatter.30.cloned.1.call-update) | async-done | bytes 786448 | tf_op jit(solution)/shard_map/reduce_scatter | solution.py:45
  975.6 80.4 %reduce-scatter.34.cloned.1.call-done = f32[96,1152]{1,0:T(8,128)} async-done(((f32[768,1152]{1,0:T(8,128)}), f32[96,1152]{1,0:T(8,128)}) %reduce-scatter.34.cloned.1.call-update) | async-done | bytes 442384
  1058.6 96.8 %reduce-scatter.32.cloned.1.call-done = f32[2,96,768]{2,1,0:T(8,128)} async-done(((f32[2,768,768]{2,1,0:T(8,128)}), f32[2,96,768]{2,1,0:T(8,128)}) %reduce-scatter.32.cloned.1.call-update) | async-done | bytes 589840 | tf_op jit(solution)/shard_map/reduce_scatter | solution.py:405
  (488 shorter events, 244.6 us)
Async XLA Ops:
  7.2 103.9 %reduce-scatter.16.cloned.1.call-start = ((), (), s32[]{:S(2)}) async-start(), calls=%async_computation.11 | async-start | bytes 3932160 | tf_op jit(solution)/shard_map/reduce_scatter | solution.py:32
  7.2 8.1 collective-permute-start
  16.4 20.4 %collective-permute-start.1 = (bf16[512,768]{1,0:T(8,128)(2,1)S(1)}, bf16[512,768]{1,0:T(8,128)(2,1)}, u32[]{:S(2)}, u32[]{:S(2)}) collective-permute-start(bf16[512,768]{1,0:T(8,128)(2,1)S(1)} %pad_maximum_fusion.4), channel_id=1, source_target_pairs={{0,2},{1,3},{2,0},{3,1},{4,6},{5,7},{6,4},{7,5},{8,10},{9,11},{10,... | collective-permute-start | bytes 2359304 | tf_op jit(solution)/shard_map/ppermute | solution.py:20
  70.4 40.8 %copy-start.30 = (bf16[256,768]{1,0:T(8,128)(2,1)S(1)}, bf16[256,768]{1,0:T(8,128)(2,1)}, u32[]{:S(2)}) copy-start(bf16[256,768]{1,0:T(8,128)(2,1)} %param.23) | copy-start | bytes 1179652
  72.7 47.3 %copy-start.82 = (f32[2,768]{1,0:T(2,128)S(1)}, f32[2,768]{1,0:T(2,128)}, u32[]{:S(2)}) copy-start(f32[2,768]{1,0:T(2,128)} %param.33) | copy-start | bytes 18436
  72.7 124.0 %reduce-scatter.18.cloned.1.call-start = ((), (), s32[]{:S(2)}) async-start(), calls=%async_computation.12 | async-start | bytes 3932160 | tf_op jit(solution)/shard_map/reduce_scatter | solution.py:32
  72.9 123.8 %copy-start.55 = (f32[768]{0:T(1024)}, f32[768]{0:T(1024)S(1)}, u32[]{:S(2)}) copy-start(f32[768]{0:T(1024)S(1)} %get-tuple-element.556) | copy-start | bytes 9220
  72.9 230.5 %copy-start.57 = (f32[768]{0:T(1024)}, f32[768]{0:T(1024)S(1)}, u32[]{:S(2)}) copy-start(f32[768]{0:T(1024)S(1)} %get-tuple-element.557) | copy-start | bytes 9220
  112.5 84.3 %copy-start = (f32[256,768]{1,0:T(8,128)}, f32[256,768]{1,0:T(8,128)S(1)}, u32[]{:S(2)}) copy-start(f32[256,768]{1,0:T(8,128)S(1)} %get-tuple-element.521) | copy-start | bytes 2359300
  112.5 84.2 %copy-start.59 = (f32[256]{0:T(256)}, f32[256]{0:T(256)S(1)}, u32[]{:S(2)}) copy-start(f32[256]{0:T(256)S(1)} %broadcast_multiply_fusion.11) | copy-start | bytes 3076
  112.7 84.0 %copy-start.63 = (f32[256]{0:T(256)}, f32[256]{0:T(256)S(1)}, u32[]{:S(2)}) copy-start(f32[256]{0:T(256)S(1)} %add_rsqrt_fusion.3) | copy-start | bytes 3076
  112.9 5.5 collective-permute-start.2
  118.5 19.8 %collective-permute-start.3 = (bf16[512,768]{1,0:T(8,128)(2,1)S(1)}, bf16[512,768]{1,0:T(8,128)(2,1)S(1)}, u32[]{:S(2)}, u32[]{:S(2)}) collective-permute-start(bf16[512,768]{1,0:T(8,128)(2,1)S(1)} %pad_maximum_fusion.5), channel_id=1, source_target_pairs={{0,2},{1,3},{2,0},{3,1},{4,6},{5,7},{6,4},{7,5},{8,10},{9,11},{10,... | collective-permute-start | bytes 2359304 | tf_op jit(solution)/shard_map/ppermute | solution.py:20
  157.1 146.3 %reduce-scatter.20.cloned.1.call-start = ((), (), s32[]{:S(2)}) async-start(), calls=%async_computation.13 | async-start | bytes 3932160 | tf_op jit(solution)/shard_map/reduce_scatter | solution.py:32
  198.2 105.2 %copy-start.2 = (f32[256,768]{1,0:T(8,128)}, f32[256,768]{1,0:T(8,128)S(1)}, u32[]{:S(2)}) copy-start(f32[256,768]{1,0:T(8,128)S(1)} %get-tuple-element.517) | copy-start | bytes 2359300
  198.2 105.2 %copy-start.61 = (f32[256]{0:T(256)}, f32[256]{0:T(256)S(1)}, u32[]{:S(2)}) copy-start(f32[256]{0:T(256)S(1)} %broadcast_multiply_fusion.10) | copy-start | bytes 3076
  198.5 105.0 %copy-start.65 = (f32[256]{0:T(256)}, f32[256]{0:T(256)S(1)}, u32[]{:S(2)}) copy-start(f32[256]{0:T(256)S(1)} %add_rsqrt_fusion.2) | copy-start | bytes 3076
  198.7 5.6 collective-permute-start.4
  204.3 19.9 %collective-permute-start.5 = (bf16[512,768]{1,0:T(8,128)(2,1)S(1)}, bf16[512,768]{1,0:T(8,128)(2,1)}, u32[]{:S(2)}, u32[]{:S(2)}) collective-permute-start(bf16[512,768]{1,0:T(8,128)(2,1)S(1)} %pad_maximum_fusion.6), channel_id=1, source_target_pairs={{0,2},{1,3},{2,0},{3,1},{4,6},{5,7},{6,4},{7,5},{8,10},{9,11},{10,... | collective-permute-start | bytes 2359304 | tf_op jit(solution)/shard_map/ppermute | solution.py:20
  263.9 125.4 %reduce-scatter.22.cloned.1.call-start = ((), (), s32[]{:S(2)}) async-start(), calls=%async_computation.14 | async-start | bytes 3932160 | tf_op jit(solution)/shard_map/reduce_scatter | solution.py:32
  305.4 5.8 collective-permute-start.6
  311.2 19.7 %collective-permute-start.7 = (bf16[512,768]{1,0:T(8,128)(2,1)S(1)}, bf16[512,768]{1,0:T(8,128)(2,1)S(1)}, u32[]{:S(2)}, u32[]{:S(2)}) collective-permute-start(bf16[512,768]{1,0:T(8,128)(2,1)S(1)} %pad_maximum_fusion.7), channel_id=1, source_target_pairs={{0,2},{1,3},{2,0},{3,1},{4,6},{5,7},{6,4},{7,5},{8,10},{9,11},{10,... | collective-permute-start | bytes 2359304 | tf_op jit(solution)/shard_map/ppermute | solution.py:20
  349.6 41.4 %copy-start.52 = (bf16[256,768]{1,0:T(8,128)(2,1)S(1)}, bf16[256,768]{1,0:T(8,128)(2,1)}, u32[]{:S(2)}) copy-start(bf16[256,768]{1,0:T(8,128)(2,1)} %param.24) | copy-start | bytes 1179652
  349.7 64.7 %all-gather.5.cloned.1.call-start = ((), (), s32[]{:S(2)}) async-start(), calls=%async_computation.15 | async-start | bytes 1966080 | tf_op jit(solution)/shard_map/all_gather | solution.py:41
  394.6 72.0 %reduce-scatter.24.cloned.1.call-start = ((), (), s32[]{:S(2)}) async-start(), calls=%async_computation.16 | async-start | bytes 3932160 | tf_op jit(solution)/shard_map/reduce_scatter | solution.py:45
  428.5 62.7 %all-gather.7.cloned.1.call-start = ((), (), s32[]{:S(2)}) async-start(), calls=%async_computation.17 | async-start | bytes 1966080 | tf_op jit(solution)/shard_map/all_gather | solution.py:41
  471.4 121.5 %reduce-scatter.26.cloned.1.call-start = ((), (), s32[]{:S(2)}) async-start(), calls=%async_computation.18 | async-start | bytes 3932160 | tf_op jit(solution)/shard_map/reduce_scatter | solution.py:45
  554.8 38.2 %copy-start.66 = (f32[256]{0:T(256)S(1)}, f32[256]{0:T(256)}, u32[]{:S(2)}) copy-start(f32[256]{0:T(256)} %copy-done.65) | copy-start | bytes 3076
  554.8 61.8 %copy-start.85 = (f32[768]{0:T(1024)S(1)}, f32[768]{0:T(1024)}, u32[]{:S(2)}) copy-start(f32[768]{0:T(1024)} %copy-done.84) | copy-start | bytes 9220
  554.8 61.8 %all-gather.9.cloned.1.call-start = ((), (), s32[]{:S(2)}) async-start(), calls=%async_computation.19 | async-start | bytes 1966080 | tf_op jit(solution)/shard_map/all_gather | solution.py:41
  596.8 72.0 %reduce-scatter.28.cloned.1.call-start = ((), (), s32[]{:S(2)}) async-start(), calls=%async_computation.20 | async-start | bytes 3932160 | tf_op jit(solution)/shard_map/reduce_scatter | solution.py:45
  630.6 38.2 %copy-start.1 = (f32[256,768]{1,0:T(8,128)S(1)}, f32[256,768]{1,0:T(8,128)}, u32[]{:S(2)}) copy-start(f32[256,768]{1,0:T(8,128)} %copy-done) | copy-start | bytes 2359300
  630.6 38.2 %copy-start.56 = (f32[768]{0:T(1024)S(1)}, f32[768]{0:T(1024)}, u32[]{:S(2)}) copy-start(f32[768]{0:T(1024)} %copy-done.55) | copy-start | bytes 9220
  630.6 38.2 %copy-start.60 = (f32[256]{0:T(256)S(1)}, f32[256]{0:T(256)}, u32[]{:S(2)}) copy-start(f32[256]{0:T(256)} %copy-done.59) | copy-start | bytes 3076
  630.6 38.2 %copy-start.64 = (f32[256]{0:T(256)S(1)}, f32[256]{0:T(256)}, u32[]{:S(2)}) copy-start(f32[256]{0:T(256)} %copy-done.63) | copy-start | bytes 3076
  630.6 43.0 %copy-start.90 = (bf16[1024,768]{1,0:T(8,128)(2,1)S(1)}, bf16[1024,768]{1,0:T(8,128)(2,1)}, u32[]{:S(2)}) copy-start(bf16[1024,768]{1,0:T(8,128)(2,1)} %all-gather.5.cloned.1.call-done) | copy-start | bytes 4718596
  630.7 62.7 %all-gather.11.cloned.1.call-start = ((), (), s32[]{:S(2)}) async-start(), calls=%async_computation.21 | async-start | bytes 1966080 | tf_op jit(solution)/shard_map/all_gather | solution.py:41
  673.6 193.4 %all-reduce.5.cloned.1.call-start = ((), (), s32[]{:S(2)}) async-start(), calls=%async_computation.26 | async-start | bytes 9437184
  688.8 258.2 %reduce-scatter.36.cloned.1.call-start = ((), (), s32[]{:S(2)}) async-start(), calls=%async_computation.25 | async-start | bytes 1327104
  701.9 271.6 %reduce-scatter.30.cloned.1.call-start = ((), (), s32[]{:S(2)}) async-start(), calls=%async_computation.22 | async-start | bytes 3932160 | tf_op jit(solution)/shard_map/reduce_scatter | solution.py:45
  764.4 291.7 %reduce-scatter.34.cloned.1.call-start = ((), (), s32[]{:S(2)}) async-start(), calls=%async_computation.24 | async-start | bytes 3981312
  786.3 369.0 %reduce-scatter.32.cloned.1.call-start = ((), (), s32[]{:S(2)}) async-start(), calls=%async_computation.23 | async-start | bytes 5308416 | tf_op jit(solution)/shard_map/reduce_scatter | solution.py:405
  800.7 68.2 %copy-start.77 = (f32[768]{0:T(1024)S(1)}, f32[768]{0:T(1024)}, u32[]{:S(2)}) copy-start(f32[768]{0:T(1024)} %get-tuple-element.395) | copy-start | bytes 9220
  800.7 68.2 %copy-start.78 = (f32[768]{0:T(1024)S(1)}, f32[768]{0:T(1024)}, u32[]{:S(2)}) copy-start(f32[768]{0:T(1024)} %get-tuple-element.503) | copy-start | bytes 9220
  800.7 68.2 %copy-start.76 = (f32[768]{0:T(1024)S(1)}, f32[768]{0:T(1024)}, u32[]{:S(2)}) copy-start(f32[768]{0:T(1024)} %get-tuple-element.406) | copy-start | bytes 9220
  800.7 109.1 %copy-start.19 = (f32[2,512,3,64]{1,3,2,0:T(8,128)S(1)}, f32[2,512,3,64]{1,3,2,0:T(8,128)}, u32[]{:S(2)}) copy-start(f32[2,512,3,64]{1,3,2,0:T(8,128)} %copy-done.18) | copy-start | bytes 2359300
  800.7 109.3 %copy-start.12 = (f32[1024,3,64]{0,2,1:T(8,128)S(1)}, f32[1024,3,64]{0,2,1:T(8,128)}, u32[]{:S(2)}) copy-start(f32[1024,3,64]{0,2,1:T(8,128)} %copy-done.10) | copy-start | bytes 2359300
  802.8 170.7 %copy-start.21 = (f32[256,768]{1,0:T(8,128)S(1)}, f32[256,768]{1,0:T(8,128)}, u32[]{:S(2)}) copy-start(f32[256,768]{1,0:T(8,128)} %copy-done.20) | copy-start | bytes 2359300
  (94 other events, 608.9 us)
Sparse Core Ops, SparseCore 0:
  72.8 38.2 reduce-scatter.15
  157.2 39.4 reduce-scatter.17
  264.0 39.4 reduce-scatter.19
  349.8 39.4 reduce-scatter.21
  394.7 19.6 all-gather.4
  428.6 37.9 reduce-scatter.23
  471.5 19.6 all-gather.6
  554.9 37.9 reduce-scatter.25
  596.9 19.6 all-gather.8
  630.8 37.9 reduce-scatter.27
  673.7 19.6 all-gather.10
  697.3 169.6 all-reduce.4
  870.7 63.2 reduce-scatter.35
  936.5 36.9 reduce-scatter.29
  977.0 79.0 reduce-scatter.33
  1060.1 95.1 reduce-scatter.31
